TPU v7x, 256 devices: a whole 4x4x8 slice. The times are simulated.
256 devices in a mesh: dom: 16 (over z, core), sub: 16 (over y, x).
Axes of the slice: x: 4, y: 4, z: 8, core: 2. Of those that a mesh axis runs over, the one named last changes fastest.
Arguments:
- state: bfloat16 [262144, 256], P(('dom', 'sub')), may hold values from -6 to 6
- tile_values: float32 [256, 24, 128, 128], P(('dom', 'sub')), may hold values from 0.0003125 to 0.009375
- tile_rows: int32 [256, 24], P(('dom', 'sub')), may hold values from 0 to 7, as said below
- tile_columns: int32 [256, 24], P(('dom', 'sub')), may hold values from 0 to 7, as said below
- tile_counts: int32 [256], P(('dom', 'sub')), may hold values from 8 to 24, as said below
- send_nodes: int32 [256, 4, 256], P(('dom', 'sub')), may hold values from 0 to 1023
- face_counts: int32 [256, 4], P(('dom', 'sub')), may hold values from 0 to 256, as said below
- capacity: float32 [262144], P(('dom', 'sub')), may hold values from 0.05 to 2
- source: float32 [262144], P(('dom', 'sub')), may hold values from -12 to 12
- w_self: bfloat16 [2, 256, 256], replicated, may hold values from -0.375 to 0.375
- w_neighbour: bfloat16 [2, 256, 256], replicated, may hold values from -0.375 to 0.375
- w_out: bfloat16 [2, 256, 256], replicated, may hold values from -0.375 to 0.375
- gains: float32 [2, 2, 256], replicated, may hold values from 0.25 to 1.75
- bias: float32 [2, 256], replicated, may hold values from -3 to 3
- w_decode: float32 [256], replicated, may hold values from -0.375 to 0.375
Outputs:
- heat_level_field: float32 [262144], P(('dom', 'sub'))
- equation_defect: float32 [262144], P(('dom', 'sub'))
Inputs may be any that keep to these rules, and one draw needn't show every extreme that they name: `tile_counts`: slots at or beyond a device's count are ignored; some device has all 24 slots live. `tile_rows`: slot t < 8 names tile t, in tile_columns as well. `tile_columns`: slot t < 8 names tile t, in tile_rows as well. `face_counts`: two neighbouring devices give each other the same count; the count is 0 toward a side where the slice has no neighbour; some pair of neighbours fills all 256 slots.
All inputs are finite; a program needn't handle non-finite values.
Results may differ from a plain program's by a relative error of at most 0.005.
Values may be sent and summed in bfloat16 or wider, within the bound.
A program may use at most 64 MiB of HBM per device.

v0:
```python
import functools

import jax
import jax.numpy as jnp
from jax import lax
from jax.experimental import pallas as pl
from jax.experimental.pallas import tpu as pltpu
from jax.sharding import PartitionSpec as P

LAYERS = 2
ITERS = 3
ROUNDS = ITERS + 1
MESH = pl.DeviceIdType.MESH
F32 = jnp.float32
BF16 = jnp.bfloat16


def assemble_kernel(counts, rows, columns, tiles, high, low, total):
    groups, size = total.shape[0], total.shape[2]
    for i in range(groups):
        for j in range(groups):
            if i != j:
                total[i, j] = jnp.zeros((size, size), F32)
    for t in range(groups):
        tile = tiles[t]
        total[t, t] = tile + tile.T

    def add(t, carry):
        r, c = rows[0, t], columns[0, t]
        tile = tiles[t]
        total[r, c] += tile
        total[c, r] += tile.T
        return carry

    lax.fori_loop(groups, counts[0], add, 0)
    for i in range(groups):
        for j in range(groups):
            block = total[i, j]
            upper = block.astype(BF16)
            at = (slice(i * size, (i + 1) * size), slice(j * size, (j + 1) * size))
            high[at] = upper
            low[at] = (block - upper.astype(F32)).astype(BF16)


def assemble(tiles, rows, columns, counts, groups):
    slots, size = tiles.shape[0], tiles.shape[1]
    nodes = groups * size
    smem = pl.BlockSpec(memory_space=pltpu.SMEM)
    vmem = pl.BlockSpec(memory_space=pltpu.VMEM)
    return pl.pallas_call(
        assemble_kernel,
        out_shape=[jax.ShapeDtypeStruct((nodes, nodes), BF16)] * 2,
        in_specs=[smem, smem, smem, vmem],
        out_specs=[vmem, vmem],
        scratch_shapes=[pltpu.VMEM((groups, groups, size, size), F32)],
        compiler_params=pltpu.CompilerParams(vmem_limit_bytes=20 << 20),
        name="assemble",
    )(counts, rows, columns, tiles)


def dot(a, b):
    return jnp.dot(a, b, preferred_element_type=F32)


def parts_of(v):
    at = lax.broadcasted_iota(jnp.int32, v.shape, 0)
    first = v.astype(BF16).astype(F32)
    rest = v - first
    second = rest.astype(BF16).astype(F32)
    third = rest - second
    picked = jnp.where(at == 0, first, jnp.where(at == 1, second, jnp.where(at == 2, third, 0.0)))
    return picked.astype(BF16)


def joined(rows):
    return jnp.broadcast_to(jnp.sum(rows, axis=0, keepdims=True), rows.shape)


def spread(row):
    return jnp.broadcast_to(row, (8, row.shape[1]))


def rooted(v, gain):
    return v * lax.rsqrt(jnp.mean(v * v, axis=-1, keepdims=True) + 1e-06) * gain


def galerkin_weights(gram):
    matrix = [[gram(i, j) - gram(i, j + 1) for j in range(ITERS)] for i in range(ITERS)]
    right = [gram(i, 0) for i in range(ITERS)]
    for i in range(ITERS):
        for k in range(i + 1, ITERS):
            factor = matrix[i][k] / matrix[i][i]
            for j in range(k, ITERS):
                matrix[k][j] = matrix[k][j] - factor * matrix[i][j]
            right[k] = right[k] - factor * right[i]
    weights = [None] * ITERS
    for i in reversed(range(ITERS)):
        total = right[i]
        for j in range(i + 1, ITERS):
            total = total - matrix[i][j] * weights[j]
        weights[i] = total / matrix[i][i]
    return weights


def solve_kernel(
    n_dom,
    n_sub,
    faces,
    send_ref,
    state,
    high,
    low,
    capacity,
    source,
    w_self,
    w_neighbour,
    w_out,
    gains,
    bias,
    w_decode,
    heat_ref,
    defect_ref,
    pick,
    place,
    latents,
    own,
    inverse,
    row_out,
    row_in,
    face_out,
    face_in,
    dom_sums,
    sub_sums,
    row_send,
    row_recv,
    face_send,
    face_recv,
    dom_send,
    dom_recv,
    sub_send,
    sub_recv,
):
    dom, sub = lax.axis_index("dom"), lax.axis_index("sub")
    nodes, width = state.shape
    slots = send_ref.shape[1]
    chunk = 256
    sides = (
        (dom > 0, (dom - 1, sub)),
        (dom < n_dom - 1, (dom + 1, sub)),
        (sub > 0, (dom, sub - 1)),
        (sub < n_sub - 1, (dom, sub + 1)),
    )
    order = (2, 3, 1, 0)

    barrier = pltpu.get_barrier_semaphore()
    for r in range(1, n_dom):
        pl.semaphore_signal(barrier, inc=1, device_id=(lax.rem(dom + r, n_dom), sub), device_id_type=MESH)
    for r in range(1, n_sub):
        pl.semaphore_signal(barrier, inc=1, device_id=(dom, lax.rem(sub + r, n_sub)), device_id_type=MESH)

    position = lax.broadcasted_iota(jnp.int32, (8, slots), 1)
    for k in range(4):
        wanted = jnp.broadcast_to(send_ref[k : k + 1, :], (8, slots))
        wanted = jnp.where(position < faces[0, k], wanted, -1).astype(F32)
        node = lax.broadcasted_iota(jnp.int32, (nodes, slots), 0).astype(F32)
        place[:, k * slots : (k + 1) * slots] = (
            jnp.where(node == wanted[0:1, :], 1.0, 0.0).astype(BF16)
        )
        upright = wanted.T[:, 0:1]
        node = lax.broadcasted_iota(jnp.int32, (slots, nodes), 1).astype(F32)
        pick[k * slots : (k + 1) * slots, :] = jnp.where(node == upright, 1.0, 0.0).astype(BF16)

    for k, (there, _) in enumerate(sides):

        @pl.when(jnp.logical_not(there))
        def _():
            for layer in range(LAYERS):
                row_in[layer, k] = jnp.zeros((slots, width), BF16)
            for step in range(ROUNDS):
                face_in[step, k] = jnp.zeros((1, slots), F32)

    def row_copy(layer, k):
        return pltpu.make_async_remote_copy(
            src_ref=row_out.at[layer, k],
            dst_ref=row_in.at[layer, k ^ 1],
            send_sem=row_send.at[layer, k],
            recv_sem=row_recv.at[layer, k ^ 1],
            device_id=sides[k][1],
            device_id_type=MESH,
        )

    def row_arrival(layer, k):
        return pltpu.make_async_remote_copy(
            src_ref=row_out.at[layer, k],
            dst_ref=row_in.at[layer, k],
            send_sem=row_send.at[layer, k],
            recv_sem=row_recv.at[layer, k],
            device_id=sides[k][1],
            device_id_type=MESH,
        )

    def face_copy(step, k):
        return pltpu.make_async_remote_copy(
            src_ref=face_out.at[step, k],
            dst_ref=face_in.at[step, k ^ 1],
            send_sem=face_send.at[step, k],
            recv_sem=face_recv.at[step, k ^ 1],
            device_id=sides[k][1],
            device_id_type=MESH,
        )

    def face_arrival(step, k):
        return pltpu.make_async_remote_copy(
            src_ref=face_out.at[step, k],
            dst_ref=face_in.at[step, k],
            send_sem=face_send.at[step, k],
            recv_sem=face_recv.at[step, k],
            device_id=sides[k][1],
            device_id_type=MESH,
        )

    for layer in range(LAYERS):
        now = state if layer == 0 else latents
        for k in order:
            row_out[layer, k] = dot(pick[k * slots : (k + 1) * slots, :], now[...]).astype(BF16)
            if layer == 0 and k == order[0]:
                pl.semaphore_wait(barrier, n_dom + n_sub - 2)

            @pl.when(sides[k][0])
            def _():
                row_copy(layer, k).start()

        if layer == 0:
            ones = jnp.ones((nodes, 128), BF16)

            def count(b, carry):
                at = pl.ds(pl.multiple_of(b * chunk, chunk), chunk)
                inverse[at, :] = 1.0 / (
                    dot(high[at, :], ones) + dot(low[at, :], ones) + dot(place[at, :], ones)
                )
                return carry

            lax.fori_loop(0, nodes // chunk, count, 0)

        def before(b, carry):
            at = pl.ds(pl.multiple_of(b * chunk, chunk), chunk)
            normed = rooted(now[at, :].astype(F32), gains[layer, 0:1, :]).astype(BF16)
            own[1, at, :] = dot(normed, w_self[layer]) + bias[layer : layer + 1, :]
            own[0, at, :] = dot(high[at, :], now[...])
            return carry

        lax.fori_loop(0, nodes // chunk, before, 0)
        for k in order:

            @pl.when(sides[k][0])
            def _():
                row_arrival(layer, k).wait_recv()

        arrived = row_in.at[layer]

        def after(b, carry):
            at = pl.ds(pl.multiple_of(b * chunk, chunk), chunk)
            coupled = own[0, at, :]
            for k in range(4):
                coupled = coupled + dot(place[at, k * slots : (k + 1) * slots], arrived[k])
            mean = coupled * jnp.concatenate([inverse[at, :]] * (width // 128), axis=1)
            normed = rooted(mean, gains[layer, 1:2, :]).astype(BF16)
            linear = own[1, at, :] + dot(normed, w_neighbour[layer])
            active = (linear / (1.0 + jnp.exp(-linear))).astype(BF16)
            latents[at, :] = (now[at, :].astype(F32) + dot(active, w_out[layer])).astype(BF16)
            return carry

        lax.fori_loop(0, nodes // chunk, after, 0)

    guess = joined(
        lax.dot_general(
            parts_of(spread(w_decode[...])),
            latents[...],
            (((1,), (1,)), ((), ())),
            preferred_element_type=F32,
        )
    )
    ones_row = jnp.ones((8, nodes), BF16)
    rowsum = dot(ones_row, high[...]) + dot(ones_row, low[...]) + dot(ones_row, pick[...])
    diagonal = spread(capacity[...]) + rowsum
    scaling = 1.0 / diagonal

    def couple(step, v):
        parts = parts_of(v)
        for k in order:
            face_out[step, k] = joined(dot(parts, place[:, k * slots : (k + 1) * slots]))[0:1, :]

            @pl.when(sides[k][0])
            def _():
                face_copy(step, k).start()

        local = dot(parts, high[...]) + dot(parts, low[...])
        for k in order:

            @pl.when(sides[k][0])
            def _():
                face_arrival(step, k).wait_recv()

        for k in range(4):
            local = local + dot(parts_of(spread(face_in[step, k])), pick[k * slots : (k + 1) * slots, :])
        return joined(local)

    first = scaling * (spread(source[...]) - (diagonal * guess - couple(0, guess)))
    basis = [first]
    for step in range(1, ROUNDS):
        basis.append(scaling * couple(step, basis[-1]))

    pairs = [(i, j) for i in range(ITERS) for j in range(i, ROUNDS)]
    at_row = lax.broadcasted_iota(jnp.int32, (16, 128), 0)
    at_lane = lax.broadcasted_iota(jnp.int32, (16, 128), 1)
    packed = jnp.zeros((16, 128), F32)
    weighted = [diagonal * v for v in basis]
    for n, (i, j) in enumerate(pairs):
        product = basis[i] * weighted[j]
        lanes = sum(product[0:1, c * 128 : (c + 1) * 128] for c in range(nodes // 128))
        packed = jnp.where(at_row == n, lanes, packed)
    packed = jnp.sum(packed, axis=1, keepdims=True)
    mine = jnp.sum(jnp.where(at_row == at_lane, packed, 0.0), axis=0, keepdims=True)

    dom_sums[dom] = mine

    def dom_copy(r):
        return pltpu.make_async_remote_copy(
            src_ref=dom_sums.at[dom],
            dst_ref=dom_sums.at[dom],
            send_sem=dom_send.at[r],
            recv_sem=dom_recv.at[r],
            device_id=(lax.rem(dom + r, n_dom), sub),
            device_id_type=MESH,
        )

    def sub_copy(r):
        return pltpu.make_async_remote_copy(
            src_ref=sub_sums.at[sub],
            dst_ref=sub_sums.at[sub],
            send_sem=sub_send.at[r],
            recv_sem=sub_recv.at[r],
            device_id=(dom, lax.rem(sub + r, n_sub)),
            device_id_type=MESH,
        )

    for r in range(1, n_dom):
        dom_copy(r).start()
    for r in range(1, n_dom):
        dom_copy(r).wait()
    sub_sums[sub] = jnp.sum(dom_sums[...], axis=0)
    for r in range(1, n_sub):
        sub_copy(r).start()
    for r in range(1, n_sub):
        sub_copy(r).wait()
    sums = jnp.sum(sub_sums[...], axis=0)

    lane = lax.broadcasted_iota(jnp.int32, (1, 128), 1)
    gram = {
        pair: jnp.sum(jnp.where(lane == n, sums, 0.0), axis=1, keepdims=True)
        for n, pair in enumerate(pairs)
    }
    weights = galerkin_weights(lambda i, j: gram[(min(i, j), max(i, j))])
    field, left = guess[0:1, :], basis[0][0:1, :]
    for step in range(ITERS):
        field = field + weights[step] * basis[step][0:1, :]
        left = left - weights[step] * (basis[step][0:1, :] - basis[step + 1][0:1, :])
    heat_ref[...] = field
    defect_ref[...] = diagonal[0:1, :] * left

    for k in order:

        @pl.when(sides[k][0])
        def _():
            for layer in range(LAYERS):
                row_copy(layer, k).wait_send()
            for step in range(ROUNDS):
                face_copy(step, k).wait_send()


def per_device(
    n_dom,
    n_sub,
    state,
    tile_values,
    tile_rows,
    tile_columns,
    tile_counts,
    send_nodes,
    face_counts,
    capacity,
    source,
    w_self,
    w_neighbour,
    w_out,
    gains,
    bias,
    w_decode,
):
    nodes, width = state.shape
    slots = send_nodes.shape[2]
    groups = nodes // tile_values.shape[2]
    high, low = assemble(tile_values[0], tile_rows, tile_columns, tile_counts, groups)
    smem = pl.BlockSpec(memory_space=pltpu.SMEM)
    vmem = pl.BlockSpec(memory_space=pltpu.VMEM)
    dma = pltpu.SemaphoreType.DMA
    heat, defect = pl.pallas_call(
        functools.partial(solve_kernel, n_dom, n_sub),
        out_shape=[jax.ShapeDtypeStruct((1, nodes), F32)] * 2,
        in_specs=[smem] + [vmem] * 12,
        out_specs=[vmem, vmem],
        scratch_shapes=[
            pltpu.VMEM((4 * slots, nodes), BF16),
            pltpu.VMEM((nodes, 4 * slots), BF16),
            pltpu.VMEM((nodes, width), BF16),
            pltpu.VMEM((2, nodes, width), F32),
            pltpu.VMEM((nodes, 128), F32),
            pltpu.VMEM((LAYERS, 4, slots, width), BF16),
            pltpu.VMEM((LAYERS, 4, slots, width), BF16),
            pltpu.VMEM((ROUNDS, 4, 1, slots), F32),
            pltpu.VMEM((ROUNDS, 4, 1, slots), F32),
            pltpu.VMEM((n_dom, 1, 128), F32),
            pltpu.VMEM((n_sub, 1, 128), F32),
            dma((LAYERS, 4)),
            dma((LAYERS, 4)),
            dma((ROUNDS, 4)),
            dma((ROUNDS, 4)),
            dma((n_dom,)),
            dma((n_dom,)),
            dma((n_sub,)),
            dma((n_sub,)),
        ],
        compiler_params=pltpu.CompilerParams(
            collective_id=0, has_side_effects=True, vmem_limit_bytes=32 << 20
        ),
        name="solve",
    )(
        face_counts,
        send_nodes[0],
        state,
        high,
        low,
        capacity[None, :],
        source[None, :],
        w_self,
        w_neighbour,
        w_out,
        gains,
        bias,
        w_decode[None, :],
    )
    return heat[0], defect[0]


def solution(mesh):
    return jax.shard_map(
        functools.partial(per_device, mesh.shape["dom"], mesh.shape["sub"]),
        mesh=mesh,
        in_specs=(
            P(("dom", "sub"), None),
            P(("dom", "sub"), None, None, None),
            P(("dom", "sub"), None),
            P(("dom", "sub"), None),
            P(("dom", "sub")),
            P(("dom", "sub"), None, None),
            P(("dom", "sub"), None),
            P(("dom", "sub")),
            P(("dom", "sub")),
            P(),
            P(),
            P(),
            P(),
            P(),
            P(),
        ),
        out_specs=(P(("dom", "sub")), P(("dom", "sub"))),
        check_vma=False,
    )
```

profile of v0, /device:TPU:1, one launch (start us, length us, event | category | flops | bytes accessed | tf_op | source)
XLA Modules:
  0.0 72.9 jit_solution(14621703625458912385)
XLA Ops:
  1.3 0.0 copy-start
  1.3 1.4 %copy-done = f32[1,24,128,128]{3,2,1,0:T(8,128)S(1)} copy-done((f32[1,24,128,128]{3,2,1,0:T(8,128)S(1)}, f32[1,24,128,128]{3,2,1,0:T(8,128)}, u32[]{:S(2)}) %copy-start) | copy-done | bytes 1572888
  2.7 0.0 copy-start.11
  2.7 0.7 copy-done.11
  3.3 0.0 copy-start.12
  3.3 0.7 copy-done.12
  4.0 2.7 %assemble.1 = (bf16[1024,1024]{1,0:T(8,128)(2,1)S(1)}, bf16[1024,1024]{1,0:T(8,128)(2,1)S(1)}) custom-call(s32[1]{0:T(128)S(6)} %copy.19.counts, s32[1,24]{1,0:T(1,128)S(1)} %copy-done.11, s32[1,24]{1,0:T(1,128)S(1)} %copy-done.12, f32[24,128,128]{2,1,0:T(8,128)S(1)} %bitcast.7), custom_call_target="tpu_custom_call" | custom-call | tf_op jit(solution)/shard_map/assemble/pallas_call | solution.py:50
  6.7 0.0 copy-start.1
  6.7 1.0 %copy-done.1 = bf16[1024,256]{1,0:T(8,128)(2,1)S(1)} copy-done((bf16[1024,256]{1,0:T(8,128)(2,1)S(1)}, bf16[1024,256]{1,0:T(8,128)(2,1)}, u32[]{:S(2)}) %copy-start.1) | copy-done | bytes 524312
  7.7 0.0 copy-start.2
  7.7 0.9 %copy-done.2 = bf16[2,256,256]{2,1,0:T(8,128)(2,1)S(1)} copy-done((bf16[2,256,256]{2,1,0:T(8,128)(2,1)S(1)}, bf16[2,256,256]{2,1,0:T(8,128)(2,1)}, u32[]{:S(2)}) %copy-start.2) | copy-done | bytes 262168
  8.7 0.0 copy-start.3
  8.7 0.9 %copy-done.3 = bf16[2,256,256]{2,1,0:T(8,128)(2,1)S(1)} copy-done((bf16[2,256,256]{2,1,0:T(8,128)(2,1)S(1)}, bf16[2,256,256]{2,1,0:T(8,128)(2,1)}, u32[]{:S(2)}) %copy-start.3) | copy-done | bytes 262168
  9.6 0.9 %copy-done.4 = bf16[2,256,256]{2,1,0:T(8,128)(2,1)S(1)} copy-done((bf16[2,256,256]{2,1,0:T(8,128)(2,1)S(1)}, bf16[2,256,256]{2,1,0:T(8,128)(2,1)}, u32[]{:S(2)}) %copy-start.4) | copy-done | bytes 262168
  10.6 0.7 copy-done.5
  11.2 0.7 copy-done.6
  11.9 0.7 copy-done.7
  12.6 0.7 copy-done.8
  13.3 0.7 copy-done.9
  14.0 0.7 copy-done.10
  14.7 0.7 copy-done.13
  15.3 56.4 %solve.1 = (f32[1,1024]{1,0:T(1,128)S(1)}, f32[1,1024]{1,0:T(1,128)S(1)}) custom-call(s32[1,4]{1,0:T(1,128)S(1)} %copy-done.13, s32[4,256]{1,0:T(4,128)S(1)} %bitcast.10, bf16[1024,256]{1,0:T(8,128)(2,1)S(1)} %copy-done.1, bf16[1024,1024]{1,0:T(8,128)(2,1)S(1)} %get-tuple-element.6.high, bf16[1024,1024]{1,0:T(8,128)(2,1)S(1)} %get-tuple-element.7.low, ...), custom_call_target="tpu_custom_call" | custom-call | tf_op jit(solution)/shard_map/solve/pallas_call | solution.py:407
  71.7 0.6 copy.20
  72.3 0.6 copy.21
  (8 shorter events, 0.0 us)
Async XLA Ops:
  1.3 1.4 %copy-start = (f32[1,24,128,128]{3,2,1,0:T(8,128)S(1)}, f32[1,24,128,128]{3,2,1,0:T(8,128)}, u32[]{:S(2)}) copy-start(f32[1,24,128,128]{3,2,1,0:T(8,128)} %param.16) | copy-start | bytes 4718596
  2.7 0.7 copy-start.11
  3.3 0.7 copy-start.12
  6.7 1.0 %copy-start.1 = (bf16[1024,256]{1,0:T(8,128)(2,1)S(1)}, bf16[1024,256]{1,0:T(8,128)(2,1)}, u32[]{:S(2)}) copy-start(bf16[1024,256]{1,0:T(8,128)(2,1)} %state.1) | copy-start | bytes 1572868
  7.7 0.9 %copy-start.2 = (bf16[2,256,256]{2,1,0:T(8,128)(2,1)S(1)}, bf16[2,256,256]{2,1,0:T(8,128)(2,1)}, u32[]{:S(2)}) copy-start(bf16[2,256,256]{2,1,0:T(8,128)(2,1)} %w_self.1) | copy-start | bytes 786436
  8.7 0.9 %copy-start.3 = (bf16[2,256,256]{2,1,0:T(8,128)(2,1)S(1)}, bf16[2,256,256]{2,1,0:T(8,128)(2,1)}, u32[]{:S(2)}) copy-start(bf16[2,256,256]{2,1,0:T(8,128)(2,1)} %w_neighbour.1) | copy-start | bytes 786436
  9.6 0.9 %copy-start.4 = (bf16[2,256,256]{2,1,0:T(8,128)(2,1)S(1)}, bf16[2,256,256]{2,1,0:T(8,128)(2,1)}, u32[]{:S(2)}) copy-start(bf16[2,256,256]{2,1,0:T(8,128)(2,1)} %w_out.1) | copy-start | bytes 786436
  10.6 0.7 copy-start.5
  11.2 0.7 copy-start.6
  11.9 0.7 copy-start.7
  12.6 0.7 copy-start.8
  13.3 0.7 copy-start.9
  14.0 0.7 copy-start.10
  14.7 0.7 copy-start.13
where the time goes:
time: 73.5 us; the launch traced here: 72.9 us
  Pallas kernels  59 us (80%)
  local copies, waits for them, and re-layouts  12.5 us (17%)
  between operations  1.32 us (2%)
    pallas_call x1, Pallas kernels, per_device(): pl.pallas_call(functools.partial(solve_kernel, n_dom, n_sub), out_shape=[...  56.4 us
    unnamed x30, local copies, waits for them, and re-layouts  12.5 us
    pallas_call x1, Pallas kernels, assemble(): pl.pallas_call(assemble_kernel, out_shape=[jax.ShapeDtypeStruct((nodes, n...  2.65 us

commit v1 on v0

--- a/solution.py
+++ b/solution.py
@@ -10,20 +10,53 @@
 LAYERS = 2
 ITERS = 3
 ROUNDS = ITERS + 1
+VMEM_BYTES = 67_043_328
 MESH = pl.DeviceIdType.MESH
 F32 = jnp.float32
 BF16 = jnp.bfloat16
 
 
-def assemble_kernel(counts, rows, columns, tiles, high, low, total):
+def assemble_kernel(
+    counts_hbm,
+    rows_hbm,
+    columns_hbm,
+    tiles_hbm,
+    high_hbm,
+    low_hbm,
+    counts,
+    rows,
+    columns,
+    tiles,
+    total,
+    high,
+    low,
+    sem,
+    out_sem,
+):
     groups, size = total.shape[0], total.shape[2]
+    slots = tiles.shape[0]
+    cuts = [(at, min(at + groups, slots)) for at in range(0, slots, groups)]
+    copies = [
+        pltpu.make_async_copy(tiles_hbm.at[0, lo:hi], tiles.at[lo:hi], sem.at[n])
+        for n, (lo, hi) in enumerate(cuts)
+    ]
+    small = [
+        pltpu.make_async_copy(counts_hbm, counts, sem.at[len(cuts)]),
+        pltpu.make_async_copy(rows_hbm, rows, sem.at[len(cuts) + 1]),
+        pltpu.make_async_copy(columns_hbm, columns, sem.at[len(cuts) + 2]),
+    ]
+    for copy in copies + small:
+        copy.start()
     for i in range(groups):
         for j in range(groups):
             if i != j:
                 total[i, j] = jnp.zeros((size, size), F32)
+    copies[0].wait()
     for t in range(groups):
         tile = tiles[t]
         total[t, t] = tile + tile.T
+    for copy in copies[1:] + small:
+        copy.wait()
 
     def add(t, carry):
         r, c = rows[0, t], columns[0, t]
@@ -33,6 +66,7 @@
         return carry
 
     lax.fori_loop(groups, counts[0], add, 0)
+    stores = []
     for i in range(groups):
         for j in range(groups):
             block = total[i, j]
@@ -40,20 +74,36 @@
             at = (slice(i * size, (i + 1) * size), slice(j * size, (j + 1) * size))
             high[at] = upper
             low[at] = (block - upper.astype(F32)).astype(BF16)
+        band = slice(i * size, (i + 1) * size)
+        stores.append(pltpu.make_async_copy(high.at[band], high_hbm.at[band], out_sem.at[0, i]))
+        stores.append(pltpu.make_async_copy(low.at[band], low_hbm.at[band], out_sem.at[1, i]))
+        stores[-2].start()
+        stores[-1].start()
+    for store in stores:
+        store.wait()
 
 
 def assemble(tiles, rows, columns, counts, groups):
-    slots, size = tiles.shape[0], tiles.shape[1]
+    slots, size = tiles.shape[1], tiles.shape[2]
     nodes = groups * size
-    smem = pl.BlockSpec(memory_space=pltpu.SMEM)
-    vmem = pl.BlockSpec(memory_space=pltpu.VMEM)
+    hbm = pl.BlockSpec(memory_space=pltpu.HBM)
     return pl.pallas_call(
         assemble_kernel,
         out_shape=[jax.ShapeDtypeStruct((nodes, nodes), BF16)] * 2,
-        in_specs=[smem, smem, smem, vmem],
-        out_specs=[vmem, vmem],
-        scratch_shapes=[pltpu.VMEM((groups, groups, size, size), F32)],
-        compiler_params=pltpu.CompilerParams(vmem_limit_bytes=20 << 20),
+        in_specs=[hbm] * 4,
+        out_specs=[hbm, hbm],
+        scratch_shapes=[
+            pltpu.SMEM(counts.shape, jnp.int32),
+            pltpu.SMEM(rows.shape, jnp.int32),
+            pltpu.SMEM(columns.shape, jnp.int32),
+            pltpu.VMEM((slots, size, size), F32),
+            pltpu.VMEM((groups, groups, size, size), F32),
+            pltpu.VMEM((nodes, nodes), BF16),
+            pltpu.VMEM((nodes, nodes), BF16),
+            pltpu.SemaphoreType.DMA((-(-slots // groups) + 3,)),
+            pltpu.SemaphoreType.DMA((2, groups)),
+        ],
+        compiler_params=pltpu.CompilerParams(vmem_limit_bytes=VMEM_BYTES),
         name="assemble",
     )(counts, rows, columns, tiles)
 
@@ -102,44 +152,40 @@
     return weights
 
 
-def solve_kernel(
-    n_dom,
-    n_sub,
-    faces,
-    send_ref,
-    state,
-    high,
-    low,
-    capacity,
-    source,
-    w_self,
-    w_neighbour,
-    w_out,
-    gains,
-    bias,
-    w_decode,
-    heat_ref,
-    defect_ref,
-    pick,
-    place,
-    latents,
-    own,
-    inverse,
-    row_out,
-    row_in,
-    face_out,
-    face_in,
-    dom_sums,
-    sub_sums,
-    row_send,
-    row_recv,
-    face_send,
-    face_recv,
-    dom_send,
-    dom_recv,
-    sub_send,
-    sub_recv,
-):
+def solve_kernel(n_dom, n_sub, *refs):
+    copied, refs = refs[:13], refs[13:]
+    (heat_ref, defect_ref), refs = refs[:2], refs[2:]
+    local, refs = refs[:13], refs[13:]
+    faces, send_ref, state, capacity, source, w_self, w_neighbour, w_out, gains, bias, w_decode = local[:11]
+    high, low = local[11:]
+    (
+        load,
+        pick,
+        place,
+        latents,
+        own,
+        inverse,
+        row_out,
+        row_in,
+        face_out,
+        face_in,
+        dom_sums,
+        sub_sums,
+        row_send,
+        row_recv,
+        face_send,
+        face_recv,
+        dom_send,
+        dom_recv,
+        sub_send,
+        sub_recv,
+    ) = refs
+    loads = [
+        pltpu.make_async_copy(source_ref, target, load.at[n])
+        for n, (source_ref, target) in enumerate(zip(copied, local))
+    ]
+    for n in (1, 0, 2, 11, 12, 5, 8, 9, 6, 7, 10, 3, 4):
+        loads[n].start()
     dom, sub = lax.axis_index("dom"), lax.axis_index("sub")
     nodes, width = state.shape
     slots = send_ref.shape[1]
@@ -159,16 +205,25 @@
         pl.semaphore_signal(barrier, inc=1, device_id=(dom, lax.rem(sub + r, n_sub)), device_id_type=MESH)
 
     position = lax.broadcasted_iota(jnp.int32, (8, slots), 1)
-    for k in range(4):
-        wanted = jnp.broadcast_to(send_ref[k : k + 1, :], (8, slots))
-        wanted = jnp.where(position < faces[0, k], wanted, -1).astype(F32)
-        node = lax.broadcasted_iota(jnp.int32, (nodes, slots), 0).astype(F32)
-        place[:, k * slots : (k + 1) * slots] = (
-            jnp.where(node == wanted[0:1, :], 1.0, 0.0).astype(BF16)
-        )
-        upright = wanted.T[:, 0:1]
+    loads[1].wait()
+    loads[0].wait()
+    wanted = [
+        jnp.where(
+            position < faces[0, k], jnp.broadcast_to(send_ref[k : k + 1, :], (8, slots)), -1
+        ).astype(F32)
+        for k in range(4)
+    ]
+    for k in order:
         node = lax.broadcasted_iota(jnp.int32, (slots, nodes), 1).astype(F32)
+        upright = wanted[k].T[:, 0:1]
         pick[k * slots : (k + 1) * slots, :] = jnp.where(node == upright, 1.0, 0.0).astype(BF16)
+    at_row = lax.broadcasted_iota(jnp.int32, (8, 128), 0)
+    slot_node = jnp.zeros((8, 128), jnp.int32)
+    for r in range(8):
+        lanes = slice((r % 2) * 128, (r % 2) * 128 + 128)
+        slot_node = jnp.where(at_row == r, send_ref[r // 2 : r // 2 + 1, lanes], slot_node)
+    slot_lane, slot_group = jnp.bitwise_and(slot_node, 127), jnp.right_shift(slot_node, 7)
+    loads[2].wait()
 
     for k, (there, _) in enumerate(sides):
 
@@ -177,7 +232,7 @@
             for layer in range(LAYERS):
                 row_in[layer, k] = jnp.zeros((slots, width), BF16)
             for step in range(ROUNDS):
-                face_in[step, k] = jnp.zeros((1, slots), F32)
+                face_in[step, k] = jnp.zeros((2, 128), F32)
 
     def row_copy(layer, k):
         return pltpu.make_async_remote_copy(
@@ -231,6 +286,13 @@
                 row_copy(layer, k).start()
 
         if layer == 0:
+            for k in range(4):
+                node = lax.broadcasted_iota(jnp.int32, (nodes, slots), 0).astype(F32)
+                place[:, k * slots : (k + 1) * slots] = (
+                    jnp.where(node == wanted[k][0:1, :], 1.0, 0.0).astype(BF16)
+                )
+            for n in range(3, len(loads)):
+                loads[n].wait()
             ones = jnp.ones((nodes, 128), BF16)
 
             def count(b, carry):
@@ -241,7 +303,6 @@
                 return carry
 
             lax.fori_loop(0, nodes // chunk, count, 0)
-
         def before(b, carry):
             at = pl.ds(pl.multiple_of(b * chunk, chunk), chunk)
             normed = rooted(now[at, :].astype(F32), gains[layer, 0:1, :]).astype(BF16)
@@ -250,27 +311,36 @@
             return carry
 
         lax.fori_loop(0, nodes // chunk, before, 0)
-        for k in order:
-
+        def arrive(k):
             @pl.when(sides[k][0])
             def _():
                 row_arrival(layer, k).wait_recv()
 
         arrived = row_in.at[layer]
 
-        def after(b, carry):
-            at = pl.ds(pl.multiple_of(b * chunk, chunk), chunk)
+        def side(k):
+            def add(b, carry):
+                at = pl.ds(pl.multiple_of(b * chunk, chunk), chunk)
+                own[0, at, :] += dot(place[at, k * slots : (k + 1) * slots], arrived[k])
+                return carry
+
+            lax.fori_loop(0, nodes // chunk, add, 0)
+
+        for k in (0, 1):
+            arrive(k)
+            side(k)
+        arrive(2)
+        arrive(3)
+        for b in range(nodes // chunk):
+            at = slice(b * chunk, (b + 1) * chunk)
             coupled = own[0, at, :]
-            for k in range(4):
+            for k in (2, 3):
                 coupled = coupled + dot(place[at, k * slots : (k + 1) * slots], arrived[k])
             mean = coupled * jnp.concatenate([inverse[at, :]] * (width // 128), axis=1)
             normed = rooted(mean, gains[layer, 1:2, :]).astype(BF16)
             linear = own[1, at, :] + dot(normed, w_neighbour[layer])
             active = (linear / (1.0 + jnp.exp(-linear))).astype(BF16)
             latents[at, :] = (now[at, :].astype(F32) + dot(active, w_out[layer])).astype(BF16)
-            return carry
-
-        lax.fori_loop(0, nodes // chunk, after, 0)
 
     guess = joined(
         lax.dot_general(
@@ -286,24 +356,29 @@
     scaling = 1.0 / diagonal
 
     def couple(step, v):
-        parts = parts_of(v)
+        sent = jnp.zeros((8, 128), F32)
+        for c in range(nodes // 128):
+            found = jnp.take_along_axis(v[:, c * 128 : (c + 1) * 128], slot_lane, axis=1)
+            sent = jnp.where(slot_group == c, found, sent)
         for k in order:
-            face_out[step, k] = joined(dot(parts, place[:, k * slots : (k + 1) * slots]))[0:1, :]
+            face_out[step, k] = sent[2 * k : 2 * k + 2, :]
 
             @pl.when(sides[k][0])
             def _():
                 face_copy(step, k).start()
 
-        local = dot(parts, high[...]) + dot(parts, low[...])
-        for k in order:
+        parts = parts_of(v)
+        coupled = dot(parts, high[...]) + dot(parts, low[...])
+        for k in range(4):
 
             @pl.when(sides[k][0])
             def _():
                 face_arrival(step, k).wait_recv()
 
-        for k in range(4):
-            local = local + dot(parts_of(spread(face_in[step, k])), pick[k * slots : (k + 1) * slots, :])
-        return joined(local)
+            came = face_in[step, k]
+            came = jnp.concatenate([spread(came[0:1, :]), spread(came[1:2, :])], axis=1)
+            coupled = coupled + dot(parts_of(came), pick[k * slots : (k + 1) * slots, :])
+        return joined(coupled)
 
     first = scaling * (spread(source[...]) - (diagonal * guess - couple(0, guess)))
     basis = [first]
@@ -400,16 +475,34 @@
     nodes, width = state.shape
     slots = send_nodes.shape[2]
     groups = nodes // tile_values.shape[2]
-    high, low = assemble(tile_values[0], tile_rows, tile_columns, tile_counts, groups)
-    smem = pl.BlockSpec(memory_space=pltpu.SMEM)
+    high, low = assemble(tile_values, tile_rows, tile_columns, tile_counts, groups)
+    hbm = pl.BlockSpec(memory_space=pltpu.HBM)
     vmem = pl.BlockSpec(memory_space=pltpu.VMEM)
     dma = pltpu.SemaphoreType.DMA
+    copied = (
+        face_counts,
+        send_nodes[0],
+        state,
+        capacity[None, :],
+        source[None, :],
+        w_self,
+        w_neighbour,
+        w_out,
+        gains,
+        bias,
+        w_decode[None, :],
+        high,
+        low,
+    )
     heat, defect = pl.pallas_call(
         functools.partial(solve_kernel, n_dom, n_sub),
         out_shape=[jax.ShapeDtypeStruct((1, nodes), F32)] * 2,
-        in_specs=[smem] + [vmem] * 12,
+        in_specs=[hbm] * len(copied),
         out_specs=[vmem, vmem],
-        scratch_shapes=[
+        scratch_shapes=[pltpu.SMEM(face_counts.shape, jnp.int32)]
+        + [pltpu.VMEM(array.shape, array.dtype) for array in copied[1:]]
+        + [
+            dma((len(copied),)),
             pltpu.VMEM((4 * slots, nodes), BF16),
             pltpu.VMEM((nodes, 4 * slots), BF16),
             pltpu.VMEM((nodes, width), BF16),
@@ -417,8 +510,8 @@
             pltpu.VMEM((nodes, 128), F32),
             pltpu.VMEM((LAYERS, 4, slots, width), BF16),
             pltpu.VMEM((LAYERS, 4, slots, width), BF16),
-            pltpu.VMEM((ROUNDS, 4, 1, slots), F32),
-            pltpu.VMEM((ROUNDS, 4, 1, slots), F32),
+            pltpu.VMEM((ROUNDS, 4, 2, 128), F32),
+            pltpu.VMEM((ROUNDS, 4, 2, 128), F32),
             pltpu.VMEM((n_dom, 1, 128), F32),
             pltpu.VMEM((n_sub, 1, 128), F32),
             dma((LAYERS, 4)),
@@ -431,24 +524,10 @@
             dma((n_sub,)),
         ],
         compiler_params=pltpu.CompilerParams(
-            collective_id=0, has_side_effects=True, vmem_limit_bytes=32 << 20
+            collective_id=0, has_side_effects=True, vmem_limit_bytes=VMEM_BYTES
         ),
         name="solve",
-    )(
-        face_counts,
-        send_nodes[0],
-        state,
-        high,
-        low,
-        capacity[None, :],
-        source[None, :],
-        w_self,
-        w_neighbour,
-        w_out,
-        gains,
-        bias,
-        w_decode[None, :],
-    )
+    )(*copied)
     return heat[0], defect[0]
 
 

time: 73.5 us -> 62.2 us (0.85)
  local copies, waits for them, and re-layouts: 12.5 us -> 2.54 us
    unnamed x30 -> x2, local copies, waits for them, and re-layouts: 12.5 us -> 2.54 us
    pallas_call x1, Pallas kernels: 56.4 us -> 53.9 us  [per_device(): pl.pallas_call(functools.partial(solve_kernel, n_dom, n_sub), out_shape=[...]
    pallas_call x1, Pallas kernels: 2.65 us -> 4.42 us  [assemble(): pl.pallas_call(assemble_kernel, out_shape=[jax.ShapeDtypeStruct((nodes, n...]
where the time goes in v1:
time: 62.2 us
  Pallas kernels  58.3 us (94%)
  local copies, waits for them, and re-layouts  2.54 us (4%)
  between operations  1.29 us (2%)
    pallas_call x1, Pallas kernels, per_device(): pl.pallas_call(functools.partial(solve_kernel, n_dom, n_sub), out_shape=[...  53.9 us
    pallas_call x1, Pallas kernels, assemble(): pl.pallas_call(assemble_kernel, out_shape=[jax.ShapeDtypeStruct((nodes, n...  4.42 us
    unnamed x2, local copies, waits for them, and re-layouts  2.54 us

profile of v1, /device:TPU:1, one launch (start us, length us, event | category | flops | bytes accessed | tf_op | source)
XLA Modules:
  0.0 62.2 jit_solution(9326658598490358367)
XLA Ops:
  1.3 4.4 %assemble.1 = (bf16[1024,1024]{1,0:T(8,128)(2,1)}, bf16[1024,1024]{1,0:T(8,128)(2,1)}) custom-call(s32[1]{0:T(128)S(6)} %copy.19.counts_hbm, s32[1,24]{1,0:T(1,128)} %rows_hbm.1, s32[1,24]{1,0:T(1,128)} %columns_hbm.1, f32[1,24,128,128]{3,2,1,0:T(8,128)} %tiles_hbm.1), custom_call_target="tpu_custom_call" | custom-call | tf_op jit(solution)/shard_map/assemble/pallas_call | solution.py:90
  5.7 53.9 %solve.1 = (f32[1,1024]{1,0:T(1,128)}, f32[1,1024]{1,0:T(1,128)}) custom-call(s32[1,4]{1,0:T(1,128)} %refs_0_.1, s32[4,256]{1,0:T(4,128)} %bitcast.8, bf16[1024,256]{1,0:T(8,128)(2,1)} %refs_2_.1, f32[1,1024]{1,0:T(1,128)} %bitcast.9, f32[1,1024]{1,0:T(1,128)} %bitcast.10, bf16[2,256,256]{2,1,0:T(8,128)(2,1)} %refs_5_.1, bf16[2,256,256]{2,1,0:T(8,128)(2,1)} %refs_6_.1, ...), custom_call_target="tpu_custom_call" | custom-call | tf_op jit(solution)/shard_map/solve/pallas_call | solution.py:497
  59.6 1.3 %copy.20 = f32[1024]{0:T(1024)} copy(f32[1024]{0:T(1024)} %bitcast.7) | data formatting | bytes 8192
  60.9 1.3 %copy.21 = f32[1024]{0:T(1024)} copy(f32[1024]{0:T(1024)} %bitcast.6) | data formatting | bytes 8192

commit v2 on v1

--- a/solution.py
+++ b/solution.py
@@ -16,96 +16,43 @@
 BF16 = jnp.bfloat16
 
 
-def assemble_kernel(
-    counts_hbm,
-    rows_hbm,
-    columns_hbm,
-    tiles_hbm,
-    high_hbm,
-    low_hbm,
-    counts,
-    rows,
-    columns,
-    tiles,
-    total,
-    high,
-    low,
-    sem,
-    out_sem,
-):
-    groups, size = total.shape[0], total.shape[2]
-    slots = tiles.shape[0]
-    cuts = [(at, min(at + groups, slots)) for at in range(0, slots, groups)]
-    copies = [
-        pltpu.make_async_copy(tiles_hbm.at[0, lo:hi], tiles.at[lo:hi], sem.at[n])
-        for n, (lo, hi) in enumerate(cuts)
-    ]
-    small = [
-        pltpu.make_async_copy(counts_hbm, counts, sem.at[len(cuts)]),
-        pltpu.make_async_copy(rows_hbm, rows, sem.at[len(cuts) + 1]),
-        pltpu.make_async_copy(columns_hbm, columns, sem.at[len(cuts) + 2]),
-    ]
-    for copy in copies + small:
-        copy.start()
+def assemble(counts, rows, columns, tiles, chained, high, low):
+    slots, size = tiles.shape[0], tiles.shape[1]
+    groups = high.shape[0] // size
+    spare = slots - groups
+    chained[spare] = jnp.zeros((size, size), F32)
+    keys = []
+    for t in range(spare):
+        r, c = rows[0, groups + t], columns[0, groups + t]
+        key = jnp.where(
+            groups + t < counts[0], jnp.minimum(r, c) * groups + jnp.maximum(r, c), -1
+        )
+        before = spare
+        for u in range(t):
+            before = jnp.where(keys[u] == key, u, before)
+        keys.append(key)
+        tile = tiles[groups + t]
+        upright = jnp.where(r <= c, 1.0, 0.0)
+        chained[t] = chained[before] + (upright * tile + (1.0 - upright) * tile.T)
+
+    def put(i, j, block):
+        upper = block.astype(BF16)
+        at = (slice(i * size, (i + 1) * size), slice(j * size, (j + 1) * size))
+        high[at] = upper
+        low[at] = (block - upper.astype(F32)).astype(BF16)
+
     for i in range(groups):
-        for j in range(groups):
-            if i != j:
-                total[i, j] = jnp.zeros((size, size), F32)
-    copies[0].wait()
-    for t in range(groups):
-        tile = tiles[t]
-        total[t, t] = tile + tile.T
-    for copy in copies[1:] + small:
-        copy.wait()
-
-    def add(t, carry):
-        r, c = rows[0, t], columns[0, t]
-        tile = tiles[t]
-        total[r, c] += tile
-        total[c, r] += tile.T
-        return carry
-
-    lax.fori_loop(groups, counts[0], add, 0)
-    stores = []
-    for i in range(groups):
-        for j in range(groups):
-            block = total[i, j]
-            upper = block.astype(BF16)
-            at = (slice(i * size, (i + 1) * size), slice(j * size, (j + 1) * size))
-            high[at] = upper
-            low[at] = (block - upper.astype(F32)).astype(BF16)
-        band = slice(i * size, (i + 1) * size)
-        stores.append(pltpu.make_async_copy(high.at[band], high_hbm.at[band], out_sem.at[0, i]))
-        stores.append(pltpu.make_async_copy(low.at[band], low_hbm.at[band], out_sem.at[1, i]))
-        stores[-2].start()
-        stores[-1].start()
-    for store in stores:
-        store.wait()
-
-
-def assemble(tiles, rows, columns, counts, groups):
-    slots, size = tiles.shape[1], tiles.shape[2]
-    nodes = groups * size
-    hbm = pl.BlockSpec(memory_space=pltpu.HBM)
-    return pl.pallas_call(
-        assemble_kernel,
-        out_shape=[jax.ShapeDtypeStruct((nodes, nodes), BF16)] * 2,
-        in_specs=[hbm] * 4,
-        out_specs=[hbm, hbm],
-        scratch_shapes=[
-            pltpu.SMEM(counts.shape, jnp.int32),
-            pltpu.SMEM(rows.shape, jnp.int32),
-            pltpu.SMEM(columns.shape, jnp.int32),
-            pltpu.VMEM((slots, size, size), F32),
-            pltpu.VMEM((groups, groups, size, size), F32),
-            pltpu.VMEM((nodes, nodes), BF16),
-            pltpu.VMEM((nodes, nodes), BF16),
-            pltpu.SemaphoreType.DMA((-(-slots // groups) + 3,)),
-            pltpu.SemaphoreType.DMA((2, groups)),
-        ],
-        compiler_params=pltpu.CompilerParams(vmem_limit_bytes=VMEM_BYTES),
-        name="assemble",
-    )(counts, rows, columns, tiles)
+        for j in range(i, groups):
+            last = spare
+            for u in range(spare):
+                last = jnp.where(keys[u] == i * groups + j, u, last)
+            block = chained[last]
+            if i == j:
+                block = block + tiles[i]
+                put(i, i, block + block.T)
+            else:
+                put(i, j, block)
+                put(j, i, block.T)
 
 
 def dot(a, b):
@@ -153,18 +100,22 @@
 
 
 def solve_kernel(n_dom, n_sub, *refs):
-    copied, refs = refs[:13], refs[13:]
+    copied, refs = refs[:15], refs[15:]
     (heat_ref, defect_ref), refs = refs[:2], refs[2:]
-    local, refs = refs[:13], refs[13:]
+    local, refs = refs[:15], refs[15:]
     faces, send_ref, state, capacity, source, w_self, w_neighbour, w_out, gains, bias, w_decode = local[:11]
-    high, low = local[11:]
+    tiles, rows, columns, counts = local[11:]
     (
         load,
+        chained,
+        high,
+        low,
         pick,
         place,
         latents,
         own,
         inverse,
+        diagonal_ref,
         row_out,
         row_in,
         face_out,
@@ -184,7 +135,7 @@
         pltpu.make_async_copy(source_ref, target, load.at[n])
         for n, (source_ref, target) in enumerate(zip(copied, local))
     ]
-    for n in (1, 0, 2, 11, 12, 5, 8, 9, 6, 7, 10, 3, 4):
+    for n in (1, 0, 2, 12, 13, 14, 11, 5, 8, 9, 3, 6, 7, 10, 4):
         loads[n].start()
     dom, sub = lax.axis_index("dom"), lax.axis_index("sub")
     nodes, width = state.shape
@@ -293,24 +244,21 @@
                 )
             for n in range(3, len(loads)):
                 loads[n].wait()
-            ones = jnp.ones((nodes, 128), BF16)
-
-            def count(b, carry):
-                at = pl.ds(pl.multiple_of(b * chunk, chunk), chunk)
-                inverse[at, :] = 1.0 / (
-                    dot(high[at, :], ones) + dot(low[at, :], ones) + dot(place[at, :], ones)
-                )
-                return carry
-
-            lax.fori_loop(0, nodes // chunk, count, 0)
-        def before(b, carry):
-            at = pl.ds(pl.multiple_of(b * chunk, chunk), chunk)
+            assemble(counts, rows, columns, tiles, chained, high, low)
+            ones = jnp.ones((8, nodes), BF16)
+            rowsum = dot(ones, high[...]) + dot(ones, low[...]) + dot(ones, pick[...])
+            flipped = 1.0 / rowsum
+            for c in range(nodes // 128):
+                at = slice(c * 128, (c + 1) * 128)
+                inverse[at, :] = jnp.broadcast_to(flipped[:, at].T[:, 0:1], (128, 128))
+            diagonal_ref[...] = spread(capacity[...]) + rowsum
+
+        for b in range(nodes // chunk):
+            at = slice(b * chunk, (b + 1) * chunk)
             normed = rooted(now[at, :].astype(F32), gains[layer, 0:1, :]).astype(BF16)
             own[1, at, :] = dot(normed, w_self[layer]) + bias[layer : layer + 1, :]
             own[0, at, :] = dot(high[at, :], now[...])
-            return carry
-
-        lax.fori_loop(0, nodes // chunk, before, 0)
+
         def arrive(k):
             @pl.when(sides[k][0])
             def _():
@@ -319,12 +267,9 @@
         arrived = row_in.at[layer]
 
         def side(k):
-            def add(b, carry):
-                at = pl.ds(pl.multiple_of(b * chunk, chunk), chunk)
+            for b in range(nodes // chunk):
+                at = slice(b * chunk, (b + 1) * chunk)
                 own[0, at, :] += dot(place[at, k * slots : (k + 1) * slots], arrived[k])
-                return carry
-
-            lax.fori_loop(0, nodes // chunk, add, 0)
 
         for k in (0, 1):
             arrive(k)
@@ -350,9 +295,7 @@
             preferred_element_type=F32,
         )
     )
-    ones_row = jnp.ones((8, nodes), BF16)
-    rowsum = dot(ones_row, high[...]) + dot(ones_row, low[...]) + dot(ones_row, pick[...])
-    diagonal = spread(capacity[...]) + rowsum
+    diagonal = diagonal_ref[...]
     scaling = 1.0 / diagonal
 
     def couple(step, v):
@@ -419,12 +362,12 @@
             device_id_type=MESH,
         )
 
-    for r in range(1, n_dom):
+    for r in sorted(range(1, n_dom), key=lambda r: -min(r, n_dom - r)):
         dom_copy(r).start()
     for r in range(1, n_dom):
         dom_copy(r).wait()
     sub_sums[sub] = jnp.sum(dom_sums[...], axis=0)
-    for r in range(1, n_sub):
+    for r in sorted(range(1, n_sub), key=lambda r: -min(r, n_sub - r)):
         sub_copy(r).start()
     for r in range(1, n_sub):
         sub_copy(r).wait()
@@ -451,6 +394,32 @@
                 row_copy(layer, k).wait_send()
             for step in range(ROUNDS):
                 face_copy(step, k).wait_send()
+
+
+def finish_kernel(heat, defect, heat_out, defect_out, sem):
+    copies = [
+        pltpu.make_async_copy(heat, heat_out, sem.at[0]),
+        pltpu.make_async_copy(defect, defect_out, sem.at[1]),
+    ]
+    for copy in copies:
+        copy.start()
+    for copy in copies:
+        copy.wait()
+
+
+def finish(heat, defect):
+    hbm = pl.BlockSpec(memory_space=pltpu.HBM)
+    vmem = pl.BlockSpec(memory_space=pltpu.VMEM)
+    heat, defect = pl.pallas_call(
+        finish_kernel,
+        out_shape=[jax.ShapeDtypeStruct(heat.shape, heat.dtype)] * 2,
+        in_specs=[vmem, vmem],
+        out_specs=[hbm, hbm],
+        scratch_shapes=[pltpu.SemaphoreType.DMA((2,))],
+        compiler_params=pltpu.CompilerParams(vmem_limit_bytes=VMEM_BYTES - (1 << 20)),
+        name="finish",
+    )(heat, defect)
+    return heat[0], defect[0]
 
 
 def per_device(
@@ -474,8 +443,8 @@
 ):
     nodes, width = state.shape
     slots = send_nodes.shape[2]
-    groups = nodes // tile_values.shape[2]
-    high, low = assemble(tile_values, tile_rows, tile_columns, tile_counts, groups)
+    tiles = tile_values[0]
+    size = tiles.shape[1]
     hbm = pl.BlockSpec(memory_space=pltpu.HBM)
     vmem = pl.BlockSpec(memory_space=pltpu.VMEM)
     dma = pltpu.SemaphoreType.DMA
@@ -491,23 +460,34 @@
         gains,
         bias,
         w_decode[None, :],
-        high,
-        low,
+        tiles,
+        tile_rows,
+        tile_columns,
+        tile_counts,
     )
+    in_smem = (face_counts, tile_rows, tile_columns, tile_counts)
     heat, defect = pl.pallas_call(
         functools.partial(solve_kernel, n_dom, n_sub),
         out_shape=[jax.ShapeDtypeStruct((1, nodes), F32)] * 2,
         in_specs=[hbm] * len(copied),
         out_specs=[vmem, vmem],
-        scratch_shapes=[pltpu.SMEM(face_counts.shape, jnp.int32)]
-        + [pltpu.VMEM(array.shape, array.dtype) for array in copied[1:]]
+        scratch_shapes=[
+            (pltpu.SMEM if any(array is one for one in in_smem) else pltpu.VMEM)(
+                array.shape, array.dtype
+            )
+            for array in copied
+        ]
         + [
             dma((len(copied),)),
+            pltpu.VMEM((tiles.shape[0] - nodes // size + 1, size, size), F32),
+            pltpu.VMEM((nodes, nodes), BF16),
+            pltpu.VMEM((nodes, nodes), BF16),
             pltpu.VMEM((4 * slots, nodes), BF16),
             pltpu.VMEM((nodes, 4 * slots), BF16),
             pltpu.VMEM((nodes, width), BF16),
             pltpu.VMEM((2, nodes, width), F32),
             pltpu.VMEM((nodes, 128), F32),
+            pltpu.VMEM((8, nodes), F32),
             pltpu.VMEM((LAYERS, 4, slots, width), BF16),
             pltpu.VMEM((LAYERS, 4, slots, width), BF16),
             pltpu.VMEM((ROUNDS, 4, 2, 128), F32),
@@ -524,11 +504,11 @@
             dma((n_sub,)),
         ],
         compiler_params=pltpu.CompilerParams(
-            collective_id=0, has_side_effects=True, vmem_limit_bytes=VMEM_BYTES
+            collective_id=0, has_side_effects=True, vmem_limit_bytes=VMEM_BYTES - 16384
         ),
         name="solve",
     )(*copied)
-    return heat[0], defect[0]
+    return finish(heat, defect)
 
 
 def solution(mesh):

time: 62.2 us -> 55.1 us (0.89)
  Pallas kernels: 58.3 us -> 53.6 us
  local copies, waits for them, and re-layouts: 2.54 us -> 0 us
    pallas_call x1, Pallas kernels: 4.42 us -> 1.3 us  [finish(): pl.pallas_call(finish_kernel, out_shape=[jax.ShapeDtypeStruct(heat.shape,...]
    unnamed x2 -> x0, local copies, waits for them, and re-layouts: 2.54 us -> none
    pallas_call x1, Pallas kernels: 53.9 us -> 52.3 us  [per_device(): pl.pallas_call(functools.partial(solve_kernel, n_dom, n_sub), out_shape=[...]
where the time goes in v2:
time: 55.1 us; the launch traced here: 54.9 us
  Pallas kernels  53.6 us (97%)
  between operations  1.29 us (2%)
    pallas_call x1, Pallas kernels, per_device(): pl.pallas_call(functools.partial(solve_kernel, n_dom, n_sub), out_shape=[...  52.3 us
    pallas_call x1, Pallas kernels, finish(): pl.pallas_call(finish_kernel, out_shape=[jax.ShapeDtypeStruct(heat.shape,...  1.3 us

profile of v2, /device:TPU:1, one launch (start us, length us, event | category | flops | bytes accessed | tf_op | source)
XLA Modules:
  0.0 54.9 jit_solution(16116064870320280007)
XLA Ops:
  1.3 52.3 %solve.1 = (f32[1,1024]{1,0:T(1,128)}, f32[1,1024]{1,0:T(1,128)}) custom-call(s32[1,4]{1,0:T(1,128)} %refs_0_.1, s32[4,256]{1,0:T(4,128)} %bitcast.8, bf16[1024,256]{1,0:T(8,128)(2,1)} %refs_2_.1, f32[1,1024]{1,0:T(1,128)} %bitcast.9, f32[1,1024]{1,0:T(1,128)} %bitcast.10, bf16[2,256,256]{2,1,0:T(8,128)(2,1)} %refs_5_.1, bf16[2,256,256]{2,1,0:T(8,128)(2,1)} %refs_6_.1, ...), custom_call_target="tpu_custom_call" | custom-call | tf_op jit(solution)/shard_map/solve/pallas_call | solution.py:469
  53.6 1.3 %finish.1 = (f32[1,1024]{1,0:T(1,128)}, f32[1,1024]{1,0:T(1,128)}) custom-call(f32[1,1024]{1,0:T(1,128)} %get-tuple-element.6.heat, f32[1,1024]{1,0:T(1,128)} %get-tuple-element.7.defect), custom_call_target="tpu_custom_call" | custom-call | tf_op jit(solution)/shard_map/finish/pallas_call | solution.py:413

commit v3 on v2

--- a/solution.py
+++ b/solution.py
@@ -140,7 +140,7 @@
     dom, sub = lax.axis_index("dom"), lax.axis_index("sub")
     nodes, width = state.shape
     slots = send_ref.shape[1]
-    chunk = 256
+    chunk = 512
     sides = (
         (dom > 0, (dom - 1, sub)),
         (dom < n_dom - 1, (dom + 1, sub)),
@@ -365,12 +365,12 @@
     for r in sorted(range(1, n_dom), key=lambda r: -min(r, n_dom - r)):
         dom_copy(r).start()
     for r in range(1, n_dom):
-        dom_copy(r).wait()
+        dom_copy(r).wait_recv()
     sub_sums[sub] = jnp.sum(dom_sums[...], axis=0)
-    for r in sorted(range(1, n_sub), key=lambda r: -min(r, n_sub - r)):
+    for r in sorted(range(1, n_sub), key=lambda r: -min(r % 4, 4 - r % 4) - min(r // 4, 4 - r // 4)):
         sub_copy(r).start()
     for r in range(1, n_sub):
-        sub_copy(r).wait()
+        sub_copy(r).wait_recv()
     sums = jnp.sum(sub_sums[...], axis=0)
 
     lane = lax.broadcasted_iota(jnp.int32, (1, 128), 1)
@@ -383,6 +383,10 @@
     for step in range(ITERS):
         field = field + weights[step] * basis[step][0:1, :]
         left = left - weights[step] * (basis[step][0:1, :] - basis[step + 1][0:1, :])
+    for r in range(1, n_dom):
+        dom_copy(r).wait_send()
+    for r in range(1, n_sub):
+        sub_copy(r).wait_send()
     heat_ref[...] = field
     defect_ref[...] = diagonal[0:1, :] * left
 

time: 55.1 us -> 53.8 us (0.976)
  Pallas kernels: 53.6 us -> 52.3 us
    pallas_call x1, Pallas kernels: 52.3 us -> 51 us  [per_device(): pl.pallas_call(functools.partial(solve_kernel, n_dom, n_sub), out_shape=[...]
where the time goes in v3:
time: 53.8 us; the launch traced here: 53.6 us
  Pallas kernels  52.3 us (97%)
  between operations  1.29 us (2%)
    pallas_call x1, Pallas kernels, per_device(): pl.pallas_call(functools.partial(solve_kernel, n_dom, n_sub), out_shape=[...  51 us
    pallas_call x1, Pallas kernels, finish(): pl.pallas_call(finish_kernel, out_shape=[jax.ShapeDtypeStruct(heat.shape,...  1.3 us

profile of v3, /device:TPU:1, one launch (start us, length us, event | category | flops | bytes accessed | tf_op | source)
XLA Modules:
  0.0 53.6 jit_solution(5379961175327598279)
XLA Ops:
  1.3 51.0 %solve.1 = (f32[1,1024]{1,0:T(1,128)}, f32[1,1024]{1,0:T(1,128)}) custom-call(s32[1,4]{1,0:T(1,128)} %refs_0_.1, s32[4,256]{1,0:T(4,128)} %bitcast.8, bf16[1024,256]{1,0:T(8,128)(2,1)} %refs_2_.1, f32[1,1024]{1,0:T(1,128)} %bitcast.9, f32[1,1024]{1,0:T(1,128)} %bitcast.10, bf16[2,256,256]{2,1,0:T(8,128)(2,1)} %refs_5_.1, bf16[2,256,256]{2,1,0:T(8,128)(2,1)} %refs_6_.1, ...), custom_call_target="tpu_custom_call" | custom-call | tf_op jit(solution)/shard_map/solve/pallas_call | solution.py:473
  52.3 1.3 %finish.1 = (f32[1,1024]{1,0:T(1,128)}, f32[1,1024]{1,0:T(1,128)}) custom-call(f32[1,1024]{1,0:T(1,128)} %get-tuple-element.6.heat, f32[1,1024]{1,0:T(1,128)} %get-tuple-element.7.defect), custom_call_target="tpu_custom_call" | custom-call | tf_op jit(solution)/shard_map/finish/pallas_call | solution.py:417
